TPU v7x, 32 devices: a whole 2x2x4 slice. The times are simulated.
32 devices in a mesh: groups: 2 (over x), kv: 16 (over z, y, core).
Axes of the slice: x: 2, y: 2, z: 4, core: 2. Of those that a mesh axis runs over, the one named last changes fastest.
Arguments:
- queries: bfloat16 [2, 64, 16384], P(None, ('groups', 'kv')), parts along dimension 1, may hold values from -90 to 90
- new_kv: bfloat16 [2, 2, 64, 1024], P(None, None, ('groups', 'kv')), parts along dimension 2, may hold values from -41 to 41
- root_kv: bfloat16 [128, 2, 128, 1024], P(('groups', 'kv')), parts along dimension 0, may hold values from -24 to 24
- branch_kv: bfloat16 [128, 2, 128, 1024], P(('groups', 'kv')), parts along dimension 0, may hold values from -24 to 24
- tail_kv: bfloat16 [64, 2, 512, 1024], P(('groups', 'kv')), parts along dimension 0, may hold values from -24 to 24
- parent: int32 [98], P('groups'), parts along dimension 0, may hold values from 0 to 16, as said below
- node_len: int32 [98], P('groups'), parts along dimension 0, may hold values from 1 to 8192, as said below
- leaf_of: int32 [64], P('groups'), parts along dimension 0, may hold values from 17 to 48, as said below
- branch_slot: int32 [128], P('groups'), parts along dimension 0, may hold values from 1 to 49, as said below
Outputs:
- attended: bfloat16 [2, 64, 16384], P(None, ('groups', 'kv')), parts along dimension 1
There are 2 independent parts, one for each index of `groups`. A program takes and returns all parts, laid end to end along the dimension named above; each array names one. Nothing has to cross between parts.
Inputs may be any that keep to these rules, and one draw needn't show every extreme that they name: Node 0 is the root and its own parent; nodes 1 to 16 are branch prefixes with parent 0; nodes 17 to 48 are private tails, each with a branch prefix as parent. At most 6 tails share a branch prefix, and some branch prefix has exactly 6. node_len[0] = 8192; a branch prefix holds 1 to 512 tokens and a tail 1 to 512; some branch prefix and some tail hold exactly those most. `leaf_of`: every tail node is the leaf of exactly one request. `branch_slot`: A branch prefix of L tokens owns exactly ceil(L / 128) slots, which hold its tokens in order of slot index, 128 to a slot, the last one partly; all other slots hold 49.
All inputs are finite; a program needn't handle non-finite values.
Results may differ from a plain program's by a relative error of at most 0.002.
Values may be sent and summed in bfloat16 or wider, within the bound.
A program may use at most 192 MiB of HBM per device.

v0:
```python
import jax
import jax.numpy as jnp
from jax import lax
from jax.sharding import PartitionSpec as P

QH = 128
KVH = 8
HD = 128
BRANCH = 16


NEG_FILL = -1e30


def block_scores(query_rows, key_rows, value_rows, live_mask):
    scale = query_rows.shape[-1] ** (-0.5)
    scores = (
        jnp.einsum("nkgd,tkd->nkgt", query_rows, key_rows, preferred_element_type=jnp.float32)
        * scale
    )
    if live_mask is not None:
        scores = jnp.where(live_mask[:, None, None, :], scores, NEG_FILL)
    peaks = jnp.max(scores, axis=-1)
    weights = jnp.exp(scores - peaks[..., None])
    if live_mask is not None:
        weights = jnp.where(live_mask[:, None, None, :], weights, 0.0)
    totals = jnp.sum(weights, axis=-1)
    outputs = jnp.einsum(
        "nkgt,tkd->nkgd",
        weights.astype(jnp.bfloat16),
        value_rows,
        preferred_element_type=jnp.float32,
    )
    return (peaks, totals, outputs)


def owned_scores(query_rows, key_rows, value_rows, live_mask):
    scale = query_rows.shape[-1] ** (-0.5)
    scores = (
        jnp.einsum("snkgd,ntkd->snkgt", query_rows, key_rows, preferred_element_type=jnp.float32)
        * scale
    )
    scores = jnp.where(live_mask[:, :, None, None, :], scores, NEG_FILL)
    peaks = jnp.max(scores, axis=-1)
    weights = jnp.exp(scores - peaks[..., None])
    weights = jnp.where(live_mask[:, :, None, None, :], weights, 0.0)
    totals = jnp.sum(weights, axis=-1)
    outputs = jnp.einsum(
        "snkgt,ntkd->snkgd",
        weights.astype(jnp.bfloat16),
        value_rows,
        preferred_element_type=jnp.float32,
    )
    return (peaks, totals, outputs)


def join_parts(earlier_part, later_part):
    peaks = jnp.maximum(earlier_part[0], later_part[0])
    scale_first = jnp.exp(earlier_part[0] - peaks)
    scale_second = jnp.exp(later_part[0] - peaks)
    totals = earlier_part[1] * scale_first + later_part[1] * scale_second
    outputs = earlier_part[2] * scale_first[..., None] + later_part[2] * scale_second[..., None]
    return (peaks, totals, outputs)


def body(queries, new_kv, root_kv, branch_kv, tail_kv, parent, node_len, leaf_of, branch_slot):
    devices = lax.axis_size("kv")
    device_index = lax.axis_index("kv")
    req_here = queries.shape[1]
    requests = req_here * devices
    heads = QH
    kv_heads = KVH
    group_size = QH // KVH
    head_dim = HD
    block_len = root_kv.shape[2]
    readers_cap = 3 * requests // BRANCH
    node_count = node_len.shape[0]
    slot_count = branch_slot.shape[0]
    slots_here = branch_kv.shape[0]
    tail_len = tail_kv.shape[2]
    slot_ids = jnp.arange(slot_count, dtype=jnp.int32)
    same_node = branch_slot[:, None] == branch_slot[None, :]
    before_slot = slot_ids[None, :] < slot_ids[:, None]
    ranks = jnp.sum((same_node & before_slot).astype(jnp.int32), axis=1)
    owner_len = node_len[jnp.minimum(branch_slot, node_count - 1)]
    filled = jnp.where(
        branch_slot < node_count, jnp.clip(owner_len - ranks * block_len, 0, block_len), 0
    )
    local_slots = device_index * slots_here + jnp.arange(slots_here, dtype=jnp.int32)
    local_node = branch_slot[local_slots]
    local_fill = filled[local_slots]
    request_ids = jnp.arange(requests, dtype=jnp.int32)
    request_branch = parent[leaf_of]
    belongs = request_branch[None, :] == local_node[:, None]
    ordering = jnp.argsort(
        jnp.where(belongs, request_ids[None, :], requests + request_ids[None, :]),
        axis=1,
        stable=True,
    )
    readers = ordering[:, :readers_cap]
    reader_live = jnp.take_along_axis(belongs, readers, axis=1)
    token_ids = jnp.arange(block_len, dtype=jnp.int32)
    own_requests = device_index * req_here + jnp.arange(req_here, dtype=jnp.int32)
    own_tail = node_len[leaf_of[own_requests]]
    root_keys = root_kv[:, 0].reshape(root_kv.shape[0] * block_len, kv_heads, head_dim)
    root_values = root_kv[:, 1].reshape(root_kv.shape[0] * block_len, kv_heads, head_dim)
    step_count = queries.shape[0]
    gathered = lax.all_gather(queries, "kv", axis=1, tiled=True)
    all_rows = gathered.reshape(step_count * requests, kv_heads, group_size, head_dim)
    state = block_scores(all_rows, root_keys, root_values, None)
    state = tuple((member.reshape((step_count, requests) + member.shape[1:]) for member in state))
    query_grid = gathered.reshape(step_count, requests, kv_heads, group_size, head_dim)
    for slot_index in range(slots_here):
        picked = readers[slot_index]
        chosen = query_grid[:, picked].reshape(
            step_count * readers_cap, kv_heads, group_size, head_dim
        )
        live_mask = reader_live[slot_index][:, None] & (token_ids < local_fill[slot_index])[None, :]
        live_mask = jnp.tile(live_mask, (step_count, 1))
        key_rows = branch_kv[slot_index, 0].reshape(block_len, kv_heads, head_dim)
        value_rows = branch_kv[slot_index, 1].reshape(block_len, kv_heads, head_dim)
        piece = block_scores(chosen, key_rows, value_rows, live_mask)
        piece = tuple(
            (member.reshape((step_count, readers_cap) + member.shape[1:]) for member in piece)
        )
        previous = tuple((member[:, picked] for member in state))
        updated = join_parts(previous, piece)
        state = tuple((member.at[:, picked].set(change) for member, change in zip(state, updated)))
    peaks = state[0].reshape(step_count, requests, heads)
    totals = state[1].reshape(step_count, requests, heads)
    normed = (state[2].reshape(step_count, requests, heads, head_dim) / totals[..., None]).astype(
        jnp.bfloat16
    )
    moved_peaks = lax.all_to_all(peaks[None], "kv", split_axis=2, concat_axis=0, tiled=True)
    moved_totals = lax.all_to_all(totals[None], "kv", split_axis=2, concat_axis=0, tiled=True)
    moved_out = lax.all_to_all(
        normed.reshape(1, step_count, requests, heads * head_dim),
        "kv",
        split_axis=2,
        concat_axis=0,
        tiled=True,
    )
    remote_peaks = jnp.max(moved_peaks, axis=0)
    factor = moved_totals * jnp.exp(moved_peaks - remote_peaks)
    summed_totals = jnp.sum(factor, axis=0)
    spread_out = (
        moved_out.reshape(devices, step_count, req_here, heads, head_dim).astype(jnp.float32)
        * factor[..., None]
    )
    summed_out = jnp.sum(spread_out, axis=0).reshape(step_count, req_here, heads * head_dim)
    remote = (
        remote_peaks.reshape(step_count, req_here, kv_heads, group_size),
        summed_totals.reshape(step_count, req_here, kv_heads, group_size),
        summed_out.reshape(step_count, req_here, kv_heads, group_size, head_dim),
    )
    own_query = queries.reshape(step_count, req_here, kv_heads, group_size, head_dim)
    tail_keys = tail_kv[:, 0].reshape(req_here, tail_len, kv_heads, head_dim)
    tail_values = tail_kv[:, 1].reshape(req_here, tail_len, kv_heads, head_dim)
    tail_live = jnp.arange(tail_len, dtype=jnp.int32)[None, :] < own_tail[:, None]
    tail_live = jnp.broadcast_to(tail_live[None], (step_count, req_here, tail_len))
    local = owned_scores(own_query, tail_keys, tail_values, tail_live)
    fresh_count = new_kv.shape[0]
    fresh_keys = jnp.swapaxes(new_kv[:, 0], 0, 1).reshape(req_here, fresh_count, kv_heads, head_dim)
    fresh_values = jnp.swapaxes(new_kv[:, 1], 0, 1).reshape(
        req_here, fresh_count, kv_heads, head_dim
    )
    step_ids = jnp.arange(step_count, dtype=jnp.int32)
    fresh_live = jnp.arange(fresh_count, dtype=jnp.int32)[None, None, :] <= step_ids[:, None, None]
    fresh_live = jnp.broadcast_to(fresh_live, (step_count, req_here, fresh_count))
    local = join_parts(local, owned_scores(own_query, fresh_keys, fresh_values, fresh_live))
    merged = join_parts(remote, local)
    result = merged[2] / merged[1][..., None]
    return result.reshape(step_count, req_here, heads * head_dim).astype(jnp.bfloat16)


def solution(mesh):
    return jax.shard_map(
        body,
        mesh=mesh,
        in_specs=(
            P(None, ("groups", "kv"), None),
            P(None, None, ("groups", "kv"), None),
            P(("groups", "kv"), None, None, None),
            P(("groups", "kv"), None, None, None),
            P(("groups", "kv"), None, None, None),
            P("groups"),
            P("groups"),
            P("groups"),
            P("groups"),
        ),
        out_specs=P(None, ("groups", "kv"), None),
        check_vma=False,
    )
```

profile of v0, /device:TPU:13, one launch (start us, length us, event | category | flops | bytes accessed | tf_op | source)
XLA Modules:
  0.0 249.3 jit_solution(17208679827013369270)
XLA Ops:
  6.5 1.8 copy.430
  9.1 1.3 gather_fusion.1
  10.4 1.4 gather_fusion
  20.9 1.8 copy.569
  22.8 1.8 fusion.122
  24.5 1.3 copy.579
  36.4 14.2 %all-gather.2.cloned.1.call-done = bf16[2,32,16384]{2,0,1:T(2,128)(2,1)} async-done(((bf16[2,2,16384]{2,0,1:T(2,128)(2,1)}), bf16[2,32,16384]{2,0,1:T(2,128)(2,1)}) %all-gather.2.cloned.1.call-update) | async-done | bytes 2097168 | tf_op jit(solution)/shard_map/all_gather | solution.py:108
  50.6 4.8 %reshape.615 = bf16[2,32,8,16,128]{4,3,2,0,1:T(8,128)(2,1)} reshape(bf16[2,32,16384]{2,0,1:T(2,128)(2,1)} %all-gather.2.cloned.1.call-done) | data formatting | bytes 4194304 | tf_op jit(solution)/shard_map/reshape | solution.py:112
  55.4 2.2 gather_fusion.6
  57.7 1.4 fusion.126
  62.1 7.1 %bitcast_reduce_fusion = (f32[64,8,16]{0,2,1:T(8,128)S(1)}, f32[8,512,64,16]{1,2,3,0:T(8,128)}) fusion(bf16[64,8,16,128]{3,2,1,0:T(8,128)(2,1)S(1)} %bitcast.360, bf16[512,8,128,1]{2,1,0,3:T(8,128)(2,1)S(1)} %bitcast.363), kind=kOutput, calls=%fused_computation.36 | convolution fusion | flops 1082122240 | bytes 19955712 | tf_op jit(solution)/shard_map/nkgd,tkd->nkgt/dot_general | solution.py:18
  69.4 10.1 %fusion.2 = (bf16[64,8,16,512]{3,0,2,1:T(8,128)(2,1)}, f32[64,8,16]{0,2,1:T(8,128)S(1)}) fusion(f32[8,512,64,16]{1,2,3,0:T(8,128)} %get-tuple-element.65, f32[64,8,16]{0,2,1:T(8,128)S(1)} %get-tuple-element.64), kind=kLoop, calls=%fused_computation.39 | loop fusion | flops 16769024 | bytes 25231360 | tf_op jit(solution)/shard_map/convert_element_type | solution.py:30
  79.6 1.3 gather_fusion.16
  80.9 1.3 gather_fusion.3
  82.2 1.3 fusion.58
  83.5 8.1 %fusion.3 = f32[8,64,16,128]{3,2,1,0:T(8,128)S(1)} fusion(bf16[64,8,16,512]{3,0,2,1:T(8,128)(2,1)} %get-tuple-element.36, bf16[512,8,128,1]{2,1,0,3:T(8,128)(2,1)S(1)} %bitcast.386), kind=kOutput, calls=%fused_computation.40 | convolution fusion | flops 1073741824 | bytes 13631488 | tf_op jit(solution)/shard_map/nkgt,tkd->nkgd/dot_general | solution.py:28
  91.7 2.5 %copy.450 = f32[2,32,8,16,128]{4,3,2,1,0:T(8,128)} copy(f32[2,32,8,16,128]{4,3,1,0,2:T(8,128)S(1)} %bitcast.364) | data formatting | bytes 8388608 | tf_op jit(solution)/shard_map/reshape | solution.py:111
  94.2 4.0 %gather_fusion.2 = f32[6,2,8,16,128]{4,3,2,1,0:T(8,128)} fusion(f32[2,32,8,16,128]{4,3,2,1,0:T(8,128)} %copy.450, s32[1024]{0:T(1024)} %copy-done.28), kind=kCustom, calls=%fused_computation.2 | custom fusion | bytes 1572888 | tf_op jit(solution)/shard_map/gather | solution.py:126
  98.8 1.8 fusion.39
  100.7 3.0 %scatter_fusion = f32[2,32,8,16,128]{4,3,2,1,0:T(8,128)} fusion(f32[2,32,8,16,128]{4,3,2,1,0:T(8,128)} %copy.450, s32[6]{0:T(128)S(1)} %copy-done.25, f32[6,2,8,16,128]{4,3,2,1,0:T(8,128)S(1)} %fusion.39), kind=kCustom, calls=%fused_computation.23 | custom fusion | bytes 2359320 | tf_op jit(solution)/shard_map/scatter | solution.py:128
  104.5 3.8 %gather_fusion.7 = f32[6,2,8,16,128]{4,3,2,1,0:T(8,128)} fusion(f32[2,32,8,16,128]{4,3,2,1,0:T(8,128)} %scatter_fusion, s32[1024]{0:T(1024)} %pad_clamp_fusion.4), kind=kCustom, calls=%fused_computation.7 | custom fusion | bytes 1572888 | tf_op jit(solution)/shard_map/gather | solution.py:126
  111.3 1.5 fusion.127
  113.3 1.4 fusion.56
  115.8 2.8 %scatter_fusion.2 = f32[2,32,8,16,128]{4,3,2,1,0:T(8,128)} fusion(f32[2,32,8,16,128]{4,3,2,1,0:T(8,128)} %scatter_fusion, s32[6]{0:T(128)S(1)} %get-tuple-element.75, f32[6,2,8,16,128]{4,3,2,1,0:T(8,128)S(1)} %fusion.37), kind=kCustom, calls=%fused_computation.25 | custom fusion | bytes 2359320 | tf_op jit(solution)/shard_map/scatter | solution.py:128
  119.2 3.7 %gather_fusion.10 = f32[6,2,8,16,128]{4,3,2,1,0:T(8,128)} fusion(f32[2,32,8,16,128]{4,3,2,1,0:T(8,128)} %scatter_fusion.2, s32[1024]{0:T(1024)S(1)} %copy-done.27), kind=kCustom, calls=%fused_computation.10 | custom fusion | bytes 1572888 | tf_op jit(solution)/shard_map/gather | solution.py:126
  125.6 1.5 fusion.128
  127.7 1.4 fusion.54
  130.2 2.8 %scatter_fusion.4 = f32[2,32,8,16,128]{4,3,2,1,0:T(8,128)} fusion(f32[2,32,8,16,128]{4,3,2,1,0:T(8,128)} %scatter_fusion.2, s32[6]{0:T(128)S(1)} %get-tuple-element.76, f32[6,2,8,16,128]{4,3,2,1,0:T(8,128)S(1)} %fusion.35), kind=kCustom, calls=%fused_computation.27 | custom fusion | bytes 2359320 | tf_op jit(solution)/shard_map/scatter | solution.py:128
  133.6 2.8 %gather_fusion.13 = f32[6,2,8,16,128]{4,3,2,1,0:T(8,128)S(1)} fusion(f32[2,32,8,16,128]{4,3,2,1,0:T(8,128)} %scatter_fusion.4, s32[1024]{0:T(1024)S(1)} %copy-done.26), kind=kCustom, calls=%fused_computation.13 | custom fusion | bytes 1572888 | tf_op jit(solution)/shard_map/gather | solution.py:126
  139.2 1.4 fusion.129
  143.2 5.7 %all-to-all-start.2 = ((f32[1,2,32,128]{3,1,0,2:T(2,128)}), f32[1,2,32,128]{3,1,0,2:T(2,128)S(1)}, u32[]{:S(2)}, u32[]{:S(2)}) async-start(f32[1,2,32,128]{3,1,0,2:T(2,128)} %copy.494), calls=%async_computation.2 | async-start | bytes 65536 | tf_op jit(solution)/shard_map/all_to_all | solution.py:134
  149.4 2.8 %scatter_fusion.6 = f32[2,32,8,16,128]{4,3,2,1,0:T(8,128)} fusion(f32[2,32,8,16,128]{4,3,2,1,0:T(8,128)} %scatter_fusion.4, s32[6]{0:T(128)S(1)} %get-tuple-element.77, f32[6,2,8,16,128]{4,3,2,1,0:T(8,128)S(1)} %fusion.33), kind=kCustom, calls=%fused_computation.29 | custom fusion | bytes 2359320 | tf_op jit(solution)/shard_map/scatter | solution.py:128
  152.2 5.0 %reshape.628 = f32[1,2,32,16384]{3,2,1,0:T(8,128)} reshape(f32[2,32,8,16,128]{4,3,2,1,0:T(8,128)} %scatter_fusion.6) | data formatting | bytes 8388608 | tf_op jit(solution)/shard_map/reshape | solution.py:131
  158.1 2.6 %div.28 = f32[2,32,128,128]{3,2,1,0:T(8,128)} broadcast(f32[2,32,128]{2,1,0:T(8,128)S(1)} %copy.488), dimensions={0,1,2} | broadcast | bytes 4227072 | tf_op jit(solution)/shard_map/div | solution.py:131
  160.7 4.9 %div.29 = f32[1,2,32,16384]{3,2,1,0:T(8,128)} reshape(f32[2,32,128,128]{3,2,1,0:T(8,128)} %div.28) | data formatting | bytes 8388608 | tf_op jit(solution)/shard_map/div | solution.py:131
  166.4 6.4 %all-to-all-start.1 = ((f32[1,2,32,128]{3,1,0,2:T(2,128)}), f32[1,2,32,128]{3,1,0,2:T(2,128)S(1)}, u32[]{:S(2)}, u32[]{:S(2)}) async-start(f32[1,2,32,128]{3,1,0,2:T(2,128)} %copy.491), calls=%async_computation.1 | async-start | bytes 65536 | tf_op jit(solution)/shard_map/all_to_all | solution.py:135
  172.7 4.0 %divide_convert_fusion = bf16[1,2,32,16384]{3,2,1,0:T(8,128)(2,1)S(1)} fusion(f32[1,2,32,16384]{3,2,1,0:T(8,128)} %reshape.628, f32[1,2,32,16384]{3,2,1,0:T(8,128)} %div.29), kind=kLoop, calls=%fused_computation.45 | loop fusion | flops 2097152 | bytes 10485760 | tf_op jit(solution)/shard_map/convert_element_type | solution.py:131
  176.8 3.6 %copy.489 = bf16[1,2,32,16384]{3,1,0,2:T(2,128)(2,1)} copy(bf16[1,2,32,16384]{3,2,1,0:T(8,128)(2,1)S(1)} %divide_convert_fusion) | data formatting | bytes 4194304 | tf_op jit(solution)/shard_map/convert_element_type | solution.py:131
  180.3 6.0 %all-to-all-start = ((bf16[1,2,32,16384]{3,1,0,2:T(2,128)(2,1)}), bf16[1,2,32,16384]{3,1,0,2:T(2,128)(2,1)S(1)}, u32[]{:S(2)}, u32[]{:S(2)}) async-start(bf16[1,2,32,16384]{3,1,0,2:T(2,128)(2,1)} %copy.489), calls=%async_computation | async-start | bytes 4194304 | tf_op jit(solution)/shard_map/all_to_all | solution.py:136
  187.8 4.6 %fusion.120 = (bf16[2,1,512,1024]{3,2,1,0:T(8,128)(2,1)}, bf16[2,1,512,1024]{3,2,1,0:T(8,128)(2,1)}) fusion(bf16[2,2,512,1024]{3,2,1,0:T(8,128)(2,1)} %param.13), kind=kLoop, calls=%fused_computation.247 | loop fusion | bytes 8388608 | tf_op jit(solution)/shard_map/slice | solution.py:158
  192.4 4.0 %copy.577 = bf16[2,1,512,1024]{2,3,0,1:T(8,128)(2,1)} copy(bf16[2,1,512,1024]{3,2,1,0:T(8,128)(2,1)} %get-tuple-element.39) | data formatting | bytes 4194304
  196.4 4.0 %copy.578 = bf16[2,1,512,1024]{2,3,0,1:T(8,128)(2,1)} copy(bf16[2,1,512,1024]{3,2,1,0:T(8,128)(2,1)} %get-tuple-element.38) | data formatting | bytes 4194304
  201.0 2.1 fusion.125
  203.7 2.6 %mul.251 = f32[16,2,2,128,128]{4,3,1,2,0:T(8,128)} broadcast(f32[16,2,2,128]{3,1,2,0:T(2,128)S(1)} %copy.496), dimensions={0,1,2,3} | broadcast | bytes 4227072 | tf_op jit(solution)/shard_map/mul | solution.py:147
  206.3 5.8 %mul.252 = f32[16,1,2,2,16384]{4,2,3,0,1:T(2,128)} reshape(f32[16,2,2,128,128]{4,3,1,2,0:T(8,128)} %mul.251) | data formatting | bytes 8388608 | tf_op jit(solution)/shard_map/mul | solution.py:147
  213.4 20.4 %all-to-all-done = bf16[1,2,32,16384]{3,1,0,2:T(2,128)(2,1)S(1)} async-done(((bf16[1,2,32,16384]{3,1,0,2:T(2,128)(2,1)}), bf16[1,2,32,16384]{3,1,0,2:T(2,128)(2,1)S(1)}, u32[]{:S(2)}, u32[]{:S(2)}) %all-to-all-start) | async-done | bytes 2097184 | tf_op jit(solution)/shard_map/all_to_all | solution.py:136
  233.8 4.8 %fusion.6 = f32[2,2,16384]{2,0,1:T(2,128)S(1)} fusion(f32[16,1,2,2,16384]{4,2,3,0,1:T(2,128)} %mul.252, bf16[1,2,16,2,16384]{4,1,3,2,0:T(2,128)(2,1)S(1)} %bitcast.359), kind=kLoop, calls=%fused_computation.44 | loop fusion | flops 3080192 | bytes 6553600 | tf_op jit(solution)/shard_map/reduce_sum | solution.py:150
  238.8 2.5 fusion.25
  (199 shorter events, 47.5 us)
Async XLA Ops:
  6.5 8.1 %copy-start = (s32[49]{0:T(128)S(1)}, s32[49]{0:T(128)}, u32[]{:S(2)}) copy-start(s32[49]{0:T(128)} %param.15) | copy-start | bytes 592
  6.5 13.4 %copy-start.7 = (bf16[4,2,128,1024]{3,2,1,0:T(8,128)(2,1)S(1)}, bf16[4,2,128,1024]{3,2,1,0:T(8,128)(2,1)}, u32[]{:S(2)}) copy-start(bf16[4,2,128,1024]{3,2,1,0:T(8,128)(2,1)} %param.12) | copy-start | bytes 6291460
  6.5 44.1 %all-gather.2.cloned.1.call-start = ((), (), s32[]{:S(2)}) async-start(), calls=%async_computation.3 | async-start | bytes 2228224 | tf_op jit(solution)/shard_map/all_gather | solution.py:108
  20.9 4.9 %copy-start.9 = (bf16[1,1,128,1024]{3,2,1,0:T(8,128)(2,1)S(1)}, bf16[1,1,128,1024]{3,2,1,0:T(8,128)(2,1)}, u32[]{:S(2)}) copy-start(bf16[1,1,128,1024]{3,2,1,0:T(8,128)(2,1)} %get-tuple-element.46) | copy-start | bytes 786436
  22.8 5.2 %copy-start.8 = (bf16[1,1,128,1024]{3,2,1,0:T(8,128)(2,1)S(1)}, bf16[1,1,128,1024]{3,2,1,0:T(8,128)(2,1)}, u32[]{:S(2)}) copy-start(bf16[1,1,128,1024]{3,2,1,0:T(8,128)(2,1)} %get-tuple-element.45) | copy-start | bytes 786436
  34.6 0.6 copy-start.24
  34.6 23.1 %copy-start.28 = (s32[1024]{0:T(1024)}, s32[1024]{0:T(1024)S(1)}, u32[]{:S(2)}) copy-start(s32[1024]{0:T(1024)S(1)} %pad_clamp_fusion.6) | copy-start | bytes 12292
  50.6 9.7 %copy-start.2 = (bf16[2,32,16384]{2,0,1:T(2,128)(2,1)S(1)}, bf16[2,32,16384]{2,0,1:T(2,128)(2,1)}, u32[]{:S(2)}) copy-start(bf16[2,32,16384]{2,0,1:T(2,128)(2,1)} %all-gather.2.cloned.1.call-done) | copy-start | bytes 6291460
  60.3 1.7 copy-start.4
  69.4 12.9 %copy-start.12 = (bf16[1,1,128,1024]{2,3,1,0:T(8,128)(2,1)S(1)}, bf16[1,1,128,1024]{2,3,1,0:T(8,128)(2,1)}, u32[]{:S(2)}) copy-start(bf16[1,1,128,1024]{2,3,1,0:T(8,128)(2,1)} %copy.570) | copy-start | bytes 786436
  69.4 14.1 %copy-start.10 = (bf16[64,8,8,128]{3,2,1,0:T(8,128)(2,1)S(1)}, bf16[64,8,8,128]{3,2,1,0:T(8,128)(2,1)}, u32[]{:S(2)}) copy-start(bf16[64,8,8,128]{3,2,1,0:T(8,128)(2,1)} %copy.581) | copy-start | bytes 3145732
  91.6 6.5 %copy-start.14 = (f32[12,8,16]{2,1,0:T(8,128)S(1)}, f32[12,8,16]{2,1,0:T(8,128)}, u32[]{:S(2)}) copy-start(f32[12,8,16]{2,1,0:T(8,128)} %copy.479) | copy-start | bytes 18436
  91.6 6.5 %copy-start.15 = (f32[6,2,8,16]{3,2,1,0:T(8,128)S(1)}, f32[6,2,8,16]{3,2,1,0:T(8,128)}, u32[]{:S(2)}) copy-start(f32[6,2,8,16]{3,2,1,0:T(8,128)} %gather_fusion.16) | copy-start | bytes 18436
  91.7 6.5 %copy-start.16 = (f32[6,2,8,16]{3,2,1,0:T(8,128)S(1)}, f32[6,2,8,16]{3,2,1,0:T(8,128)}, u32[]{:S(2)}) copy-start(f32[6,2,8,16]{3,2,1,0:T(8,128)} %gather_fusion.3) | copy-start | bytes 18436
  94.2 6.5 %copy-start.25 = (s32[6]{0:T(128)S(1)}, s32[6]{0:T(128)}, u32[]{:S(2)}) copy-start(s32[6]{0:T(128)} %copy-done.24) | copy-start | bytes 76
  94.2 9.5 %copy-start.3 = (bf16[2,32,8,16,128]{4,3,2,0,1:T(8,128)(2,1)S(1)}, bf16[2,32,8,16,128]{4,3,2,0,1:T(8,128)(2,1)}, u32[]{:S(2)}) copy-start(bf16[2,32,8,16,128]{4,3,2,0,1:T(8,128)(2,1)} %reshape.615) | copy-start | bytes 6291460
  98.8 9.4 %copy-start.21 = (f32[6,2,8,16]{3,2,1,0:T(8,128)S(1)}, f32[6,2,8,16]{3,2,1,0:T(8,128)}, u32[]{:S(2)}) copy-start(f32[6,2,8,16]{3,2,1,0:T(8,128)} %get-tuple-element.53) | copy-start | bytes 18436
  98.8 10.9 %copy-start.18 = (f32[6,2,8,16]{3,2,1,0:T(8,128)S(1)}, f32[6,2,8,16]{3,2,1,0:T(8,128)}, u32[]{:S(2)}) copy-start(f32[6,2,8,16]{3,2,1,0:T(8,128)} %get-tuple-element.31) | copy-start | bytes 18436
  111.2 4.1 %copy-start.5 = (f32[6,2,8,16,128]{4,3,2,1,0:T(8,128)S(1)}, f32[6,2,8,16,128]{4,3,2,1,0:T(8,128)}, u32[]{:S(2)}) copy-start(f32[6,2,8,16,128]{4,3,2,1,0:T(8,128)} %gather_fusion.7) | copy-start | bytes 2359300
  112.7 5.9 %copy-start.27 = (s32[1024]{0:T(1024)S(1)}, s32[1024]{0:T(1024)}, u32[]{:S(2)}) copy-start(s32[1024]{0:T(1024)} %pad_clamp_fusion.3) | copy-start | bytes 12292
  115.3 7.6 %copy-start.22 = (f32[6,2,8,16]{3,2,1,0:T(8,128)S(1)}, f32[6,2,8,16]{3,2,1,0:T(8,128)}, u32[]{:S(2)}) copy-start(f32[6,2,8,16]{3,2,1,0:T(8,128)} %get-tuple-element.52) | copy-start | bytes 18436
  115.3 8.9 %copy-start.19 = (f32[6,2,8,16]{3,2,1,0:T(8,128)S(1)}, f32[6,2,8,16]{3,2,1,0:T(8,128)}, u32[]{:S(2)}) copy-start(f32[6,2,8,16]{3,2,1,0:T(8,128)} %get-tuple-element.28) | copy-start | bytes 18436
  125.6 4.1 %copy-start.6 = (f32[6,2,8,16,128]{4,3,2,1,0:T(8,128)S(1)}, f32[6,2,8,16,128]{4,3,2,1,0:T(8,128)}, u32[]{:S(2)}) copy-start(f32[6,2,8,16,128]{4,3,2,1,0:T(8,128)} %gather_fusion.10) | copy-start | bytes 2359300
  127.1 5.9 %copy-start.26 = (s32[1024]{0:T(1024)S(1)}, s32[1024]{0:T(1024)}, u32[]{:S(2)}) copy-start(s32[1024]{0:T(1024)} %pad_clamp_fusion.2) | copy-start | bytes 12292
  129.7 6.7 %copy-start.20 = (f32[6,2,8,16]{3,2,1,0:T(8,128)S(1)}, f32[6,2,8,16]{3,2,1,0:T(8,128)}, u32[]{:S(2)}) copy-start(f32[6,2,8,16]{3,2,1,0:T(8,128)} %get-tuple-element.51) | copy-start | bytes 18436
  129.7 8.1 %copy-start.17 = (f32[6,2,8,16]{3,2,1,0:T(8,128)S(1)}, f32[6,2,8,16]{3,2,1,0:T(8,128)}, u32[]{:S(2)}) copy-start(f32[6,2,8,16]{3,2,1,0:T(8,128)} %get-tuple-element.25) | copy-start | bytes 18436
  133.6 7.6 %copy-start.11 = (bf16[1,1,128,1024]{2,3,1,0:T(8,128)(2,1)S(1)}, bf16[1,1,128,1024]{2,3,1,0:T(8,128)(2,1)}, u32[]{:S(2)}) copy-start(bf16[1,1,128,1024]{2,3,1,0:T(8,128)(2,1)} %copy.576) | copy-start | bytes 786436
  143.2 23.2 %all-to-all-start.2 = ((f32[1,2,32,128]{3,1,0,2:T(2,128)}), f32[1,2,32,128]{3,1,0,2:T(2,128)S(1)}, u32[]{:S(2)}, u32[]{:S(2)}) async-start(f32[1,2,32,128]{3,1,0,2:T(2,128)} %copy.494), calls=%async_computation.2 | async-start | bytes 65536 | tf_op jit(solution)/shard_map/all_to_all | solution.py:134
  166.4 14.0 %all-to-all-start.1 = ((f32[1,2,32,128]{3,1,0,2:T(2,128)}), f32[1,2,32,128]{3,1,0,2:T(2,128)S(1)}, u32[]{:S(2)}, u32[]{:S(2)}) async-start(f32[1,2,32,128]{3,1,0,2:T(2,128)} %copy.491), calls=%async_computation.1 | async-start | bytes 65536 | tf_op jit(solution)/shard_map/all_to_all | solution.py:135
  176.7 9.6 %copy-start.13 = (bf16[2,2,16384]{2,1,0:T(2,128)(2,1)S(1)}, bf16[2,2,16384]{2,1,0:T(2,128)(2,1)}, u32[]{:S(2)}) copy-start(bf16[2,2,16384]{2,1,0:T(2,128)(2,1)} %param.9) | copy-start | bytes 393220
  176.8 9.7 %copy-start.1 = (s32[32]{0:T(128)S(1)}, s32[32]{0:T(128)}, u32[]{:S(2)}) copy-start(s32[32]{0:T(128)} %param.16) | copy-start | bytes 388
  180.3 53.4 %all-to-all-start = ((bf16[1,2,32,16384]{3,1,0,2:T(2,128)(2,1)}), bf16[1,2,32,16384]{3,1,0,2:T(2,128)(2,1)S(1)}, u32[]{:S(2)}, u32[]{:S(2)}) async-start(bf16[1,2,32,16384]{3,1,0,2:T(2,128)(2,1)} %copy.489), calls=%async_computation | async-start | bytes 4194304 | tf_op jit(solution)/shard_map/all_to_all | solution.py:136
  192.4 4.0 %copy-start.23 = (bf16[2,2,2,1024]{3,2,1,0:T(2,128)(2,1)S(1)}, bf16[2,2,2,1024]{3,2,1,0:T(2,128)(2,1)}, u32[]{:S(2)}) copy-start(bf16[2,2,2,1024]{3,2,1,0:T(2,128)(2,1)} %param.10) | copy-start | bytes 49156
Sparse Core Ops, SparseCore 0:
  9.5 41.0 all-gather.1
where the time goes:
time: 254 us; the launch traced here: 249 us
  local copies, waits for them, and re-layouts  115 us (45%)
  other arithmetic  35.3 us (14%)
  waiting for transfers between devices  34.6 us (14%)
  matrix products  31.4 us (12%)
  starting transfers between devices  18.1 us (7%)
  between operations  14.7 us (6%)
    unnamed x72, local copies, waits for them, and re-layouts  20.7 us
    all_to_all x1, waiting for transfers between devices, body(): lax.all_to_all(normed.reshape(1, step_count, requests, heads * head_dim),...  20.4 us
    gather x12, local copies, waits for them, and re-layouts, body(): previous = tuple((member[:, picked] for member in state))  20.4 us
    scatter x14, local copies, waits for them, and re-layouts, body(): member.at[:, picked].set(change)  17.8 us
    all_gather x1, waiting for transfers between devices, body(): gathered = lax.all_gather(queries, 'kv', axis=1, tiled=True)  14.2 us
    dot_general x5, matrix products, block_scores(): jnp.einsum('nkgd,tkd->nkgt', query_rows, key_rows, preferred_element_type...  12.8 us
    dot_general x5, matrix products, block_scores(): jnp.einsum('nkgt,tkd->nkgd', weights.astype(jnp.bfloat16), value_rows, pr...  12.5 us
    convert_element_type x1, other arithmetic, block_scores(): weights.astype(jnp.bfloat16)  10.1 us
  transfers between devices with their start and end apart: 4, of which 2 were waited for; matrix products, arithmetic and copies ran while one was open for 32% of the time, Pallas kernels for 0%

commit v1 on v0

v1 whole, which is shorter than its diff:
```python
import functools

import jax
import jax.numpy as jnp
from jax import lax
from jax.experimental import pallas as pl
from jax.experimental.pallas import tpu as pltpu
from jax.sharding import PartitionSpec as P

QH = 128
KVH = 8
HD = 128
PAIR = 2
MASKED = -1e30
LOG2E = 1.4426950408889634


def attend(scores):
    unit = HD**-0.5 * LOG2E
    top = functools.reduce(jnp.maximum, [jnp.max(s, axis=0, keepdims=True) for s in scores]) * unit
    weights = [jnp.exp2(s * unit - top) for s in scores]
    total = functools.reduce(jnp.add, [jnp.sum(w, axis=0, keepdims=True) for w in weights])
    return top, total, [w.astype(jnp.bfloat16) for w in weights]


def matmul(a, b, dims):
    return lax.dot_general(a, b, (dims, ((), ())), preferred_element_type=jnp.float32)


def merge(stat_a, out_a, stat_b, out_b):
    top = jnp.maximum(stat_a[0:1], stat_b[0:1])
    wa = stat_a[1:2] * jnp.exp2(stat_a[0:1] - top)
    wb = stat_b[1:2] * jnp.exp2(stat_b[0:1] - top)
    total = wa + wb
    inv = 1.0 / total
    out = out_a.astype(jnp.float32) * (wa * inv) + out_b.astype(jnp.float32) * (wb * inv)
    return jnp.concatenate([top, total], axis=0), out


def kernel(
    devices, rows, req_here,
    q_ref, lim_ref, tl_ref, new_ref, root_hbm, branch_hbm, tail_hbm,
    out_ref,
    qbuf, root, branch, tail, vt,
    o1, s1, r1, t1, o2, s2, r2, t2, o3, s3, r3, t3, tacc, tst,
    hbm_sem, agz_s, agz_r, agy_s, agy_r, agc_s, agc_r,
    c_s, c_r, y_s, y_r, z_s, z_r,
):
    depth = devices // 4
    chunks = KVH // PAIR
    me = lax.axis_index("kv")
    core = lax.rem(me, 2)
    yy = lax.rem(me // 2, 2)
    zz = me // 4
    core_peer = me + 1 - 2 * core
    y_peer = me + 2 - 4 * yy
    n_root = root.shape[0]
    n_branch = branch.shape[0]
    quarter = depth * rows

    def z_peer(offset):
        z = lax.rem(zz + offset, depth)
        return z, z * 4 + yy * 2 + core

    loads = [
        pltpu.make_async_copy(tail_hbm, tail, hbm_sem.at[0]),
        pltpu.make_async_copy(root_hbm, root, hbm_sem.at[1]),
        pltpu.make_async_copy(branch_hbm, branch, hbm_sem.at[2]),
    ]
    for load in loads:
        load.start()

    barrier = pltpu.get_barrier_semaphore()
    for peer in [core_peer, y_peer] + [z_peer(o)[1] for o in range(1, depth)]:
        pl.semaphore_signal(
            barrier, inc=1, device_id={"kv": peer}, device_id_type=pl.DeviceIdType.MESH
        )
    pl.semaphore_wait(barrier, depth + 1)

    def remote(src, dst, send, recv, peer):
        return pltpu.make_async_remote_copy(
            src_ref=src, dst_ref=dst, send_sem=send, recv_sem=recv,
            device_id={"kv": peer}, device_id_type=pl.DeviceIdType.MESH,
        )

    def gather_z(c, o):
        return remote(
            q_ref.at[c], qbuf.at[c, core, yy, zz], agz_s.at[c, o], agz_r.at[c, o], z_peer(o)[1]
        )

    def gather_z_in(c, o):
        z = lax.rem(zz + depth - o, depth)
        return remote(
            q_ref.at[c], qbuf.at[c, core, yy, z], agz_s.at[c, o], agz_r.at[c, o], z_peer(o)[1]
        )

    def gather_y(c, y):
        return remote(qbuf.at[c, core, yy], qbuf.at[c, core, y], agy_s.at[c], agy_r.at[c], y_peer)

    def gather_c(c, half):
        return remote(qbuf.at[c, core], qbuf.at[c, half], agc_s.at[c], agc_r.at[c], core_peer)

    def send_c(c):
        return (
            remote(o1.at[c, 1 - core], r1.at[c], c_s.at[c, 0], c_r.at[c, 0], core_peer),
            remote(s1.at[c, 1 - core], t1.at[c], c_s.at[c, 1], c_r.at[c, 1], core_peer),
        )

    def send_y(c):
        return (
            remote(o2.at[c, 1 - yy], r2.at[c], y_s.at[c, 0], y_r.at[c, 0], y_peer),
            remote(s2.at[c, 1 - yy], t2.at[c], y_s.at[c, 1], y_r.at[c, 1], y_peer),
        )

    def send_z(c, o):
        z, peer = z_peer(o)
        return (
            remote(o3.at[c, z], r3.at[c, o], z_s.at[c, o, 0], z_r.at[c, o, 0], peer),
            remote(s3.at[c, z], t3.at[c, o], z_s.at[c, o, 1], z_r.at[c, o, 1], peer),
        )

    @pl.loop(0, chunks)
    def _(c):
        for o in range(1, depth):
            gather_z(c, o).start()
        qbuf[c, core, yy, zz] = q_ref[c]

    for load in loads:
        load.wait()

    def head_cols(k):
        return pl.ds(pl.multiple_of(k * HD, HD), HD)

    def tail_part(c):
        lanes = PAIR * rows
        left = lax.broadcasted_iota(jnp.int32, (1, lanes), 1) < rows
        query = [q_ref[c, h] for h in range(PAIR)]
        cols = [head_cols(c * PAIR + h) for h in range(PAIR)]
        scores = []
        for r in range(req_here):
            s = jnp.concatenate(
                [matmul(tail[r, 0, :, cols[h]], query[h], ((1,), (1,))) for h in range(PAIR)], axis=1
            )
            token = lax.broadcasted_iota(jnp.int32, s.shape, 0)
            scores.append(jnp.where(token < tl_ref[r : r + 1, :], s, MASKED))
        s = jnp.concatenate(
            [matmul(new_ref[0, :, cols[h]], query[h], ((1,), (1,))) for h in range(PAIR)], axis=1
        )
        token = lax.broadcasted_iota(jnp.int32, s.shape, 0)
        lane = lax.broadcasted_iota(jnp.int32, s.shape, 1)
        lane_req = (lane // 16) % req_here
        lane_step = (lane // (16 * req_here)) % 2
        live = (token < 2 * req_here) & (token % req_here == lane_req)
        live = live & (token // req_here <= lane_step)
        scores.append(jnp.where(live, s, MASKED))
        top, total, weights = attend(scores)
        outs = []
        for h in range(PAIR):
            values = [tail[r, 1, :, cols[h]] for r in range(req_here)] + [new_ref[1, :, cols[h]]]
            outs.append(
                functools.reduce(
                    jnp.add, [matmul(v, w, ((0,), (0,))) for v, w in zip(values, weights)]
                )
            )
        tacc[c] = jnp.where(left, outs[0], outs[1])
        tst[c] = jnp.concatenate([top, total], axis=0)

    def cache_part(c, half):
        @pl.loop(0, PAIR * 2)
        def _(i):
            h, y = i // 2, lax.rem(i, 2)
            k = c * PAIR + h
            cols = head_cols(k)
            query = qbuf[c, half, y, :, h].reshape(quarter, HD)
            scores = [matmul(root[b, 0, :, cols], query, ((1,), (1,))) for b in range(n_root)]
            for b in range(n_branch):
                s = matmul(branch[b, 0, :, cols], query, ((1,), (1,)))
                token = lax.broadcasted_iota(jnp.int32, s.shape, 0)
                scores.append(jnp.where(token < lim_ref[half, y, b : b + 1, :], s, MASKED))
            top, total, weights = attend(scores)
            out = matmul(vt[k], jnp.concatenate(weights, axis=0), ((1,), (0,)))
            o1[c, half, h, y] = (out * (1.0 / total)).astype(jnp.bfloat16)
            s1[c, half, h, y] = jnp.concatenate([top, total], axis=0)

    @pl.loop(0, KVH)
    def _(k):
        cols = head_cols(k)
        for b in range(n_root):
            vt[k, :, b * HD : (b + 1) * HD] = root[b, 1, :, cols].T
        for b in range(n_branch):
            vt[k, :, (n_root + b) * HD : (n_root + b + 1) * HD] = branch[b, 1, :, cols].T

    @pl.loop(0, chunks + 5)
    def _(t):
        @pl.when(t < chunks)
        def _():
            for o in range(1, depth):
                gather_z_in(t, o).wait_recv()
            gather_y(t, yy).start()

        @pl.when((t >= 1) & (t < chunks + 1))
        def _():
            c = t - 1
            gather_y(c, 1 - yy).wait_recv()
            gather_c(c, core).start()

        @pl.when(t < chunks // 2)
        def _():
            tail_part(2 * t)
            tail_part(2 * t + 1)

        @pl.when((t >= 2) & (t < chunks + 2))
        def _():
            c = t - 2
            gather_c(c, 1 - core).wait_recv()
            cache_part(c, 1 - core)
            for copy in send_c(c):
                copy.start()
            cache_part(c, core)

        @pl.when((t >= 3) & (t < chunks + 3))
        def _():
            c = t - 3
            for copy in send_c(c):
                copy.wait_recv()
            for y in range(2):
                for h in range(PAIR):
                    stat, out = merge(s1[c, core, h, y], o1[c, core, h, y], t1[c, h, y], r1[c, h, y])
                    o2[c, y, h] = out.astype(jnp.bfloat16)
                    s2[c, y, h] = stat
            for copy in send_y(c):
                copy.start()

        @pl.when((t >= 4) & (t < chunks + 4))
        def _():
            c = t - 4
            for copy in send_y(c):
                copy.wait_recv()
            joined = [merge(s2[c, yy, h], o2[c, yy, h], t2[c, h], r2[c, h]) for h in range(PAIR)]
            for z in range(depth):
                part = slice(z * rows, (z + 1) * rows)
                o3[c, z] = jnp.concatenate([j[1][:, part] for j in joined], axis=1).astype(
                    jnp.bfloat16
                )
                s3[c, z] = jnp.concatenate([j[0][:, part] for j in joined], axis=1)
            for o in range(1, depth):
                for copy in send_z(c, o):
                    copy.start()

        @pl.when(t >= 5)
        def _():
            c = t - 5
            for o in range(1, depth):
                for copy in send_z(c, o):
                    copy.wait_recv()
            stats = [s3[c, zz]] + [t3[c, o] for o in range(1, depth)]
            outs = [o3[c, zz]] + [r3[c, o] for o in range(1, depth)]
            own = tst[c]
            top = functools.reduce(jnp.maximum, [s[0:1] for s in stats] + [own[0:1]])
            scale = jnp.exp2(own[0:1] - top)
            number = tacc[c] * scale
            total = own[1:2] * scale
            for s, o in zip(stats, outs):
                factor = s[1:2] * jnp.exp2(s[0:1] - top)
                number = number + o.astype(jnp.float32) * factor
                total = total + factor
            out_ref[c] = (number / total).T.astype(jnp.bfloat16)

    @pl.loop(0, chunks)
    def _(c):
        for o in range(1, depth):
            gather_z(c, o).wait_send()
            for copy in send_z(c, o):
                copy.wait_send()
        gather_y(c, yy).wait_send()
        gather_c(c, core).wait_send()
        for copy in send_c(c) + send_y(c):
            copy.wait_send()


def body(queries, new_kv, root_kv, branch_kv, tail_kv, parent, node_len, leaf_of, branch_slot):
    devices = lax.axis_size("kv")
    device_index = lax.axis_index("kv")
    steps, req_here, _ = queries.shape
    requests = req_here * devices
    group = QH // KVH
    rows = steps * req_here * group
    depth = devices // 4
    quarter = depth * rows
    chunks = KVH // PAIR
    node_count = node_len.shape[0]
    slot_count = branch_slot.shape[0]
    slots_here = branch_kv.shape[0]
    block_len = branch_kv.shape[2]

    nodes = jnp.arange(node_count, dtype=jnp.int32)
    slot_ids = jnp.arange(slot_count, dtype=jnp.int32)
    local_slots = device_index * slots_here + jnp.arange(slots_here, dtype=jnp.int32)
    local_node = lax.dynamic_slice(branch_slot, (device_index * slots_here,), (slots_here,))
    before = slot_ids[None, :] < local_slots[:, None]
    ranks = jnp.sum(((branch_slot[None, :] == local_node[:, None]) & before).astype(jnp.int32), axis=1)
    owner_len = jnp.sum(jnp.where(nodes[None, :] == local_node[:, None], node_len[None, :], 0), axis=1)
    fill = jnp.clip(owner_len - ranks * block_len, 0, block_len)
    leaf_hot = leaf_of[:, None] == nodes[None, :]
    request_branch = jnp.sum(jnp.where(leaf_hot, parent[None, :], 0), axis=1)
    request_tail = jnp.sum(jnp.where(leaf_hot, node_len[None, :], 0), axis=1)
    limit = jnp.where(request_branch[None, :] == local_node[:, None], fill[:, None], 0)
    limit = limit.reshape(slots_here, depth, 2, 2, 1, req_here, 1)
    limit = jnp.broadcast_to(limit, (slots_here, depth, 2, 2, steps, req_here, group))
    limit = jnp.transpose(limit, (3, 2, 0, 1, 4, 5, 6)).reshape(2, 2, slots_here, quarter)
    own_tail = lax.dynamic_slice(request_tail, (device_index * req_here,), (req_here,))
    lane_req = (jnp.arange(PAIR * rows, dtype=jnp.int32) // group) % req_here
    tail_limit = jnp.where(
        lane_req[None, :] == jnp.arange(req_here, dtype=jnp.int32)[:, None], own_tail[:, None], 0
    )

    query = queries.reshape(steps, req_here, KVH, group, HD)
    query = jnp.transpose(query, (2, 0, 1, 3, 4)).reshape(chunks, PAIR, rows, HD)
    fresh = jnp.swapaxes(new_kv, 0, 1).reshape(2, steps * req_here, KVH * HD)
    fresh = jnp.pad(fresh, ((0, 0), (0, 16 - steps * req_here), (0, 0)))

    bf, f32 = jnp.bfloat16, jnp.float32
    vmem = pl.BlockSpec(memory_space=pltpu.VMEM)
    hbm = pl.BlockSpec(memory_space=pl.ANY)
    lanes = PAIR * rows
    tokens = (root_kv.shape[0] + slots_here) * block_len
    dma = pltpu.SemaphoreType.DMA
    out = pl.pallas_call(
        functools.partial(kernel, devices, rows, req_here),
        out_shape=jax.ShapeDtypeStruct((chunks, lanes, HD), bf),
        in_specs=[vmem] * 4 + [hbm] * 3,
        out_specs=vmem,
        scratch_shapes=[
            pltpu.VMEM((chunks, 2, 2, depth, PAIR, rows, HD), bf),
            pltpu.VMEM(root_kv.shape, bf),
            pltpu.VMEM(branch_kv.shape, bf),
            pltpu.VMEM(tail_kv.shape, bf),
            pltpu.VMEM((KVH, HD, tokens), bf),
            pltpu.VMEM((chunks, 2, PAIR, 2, HD, quarter), bf),
            pltpu.VMEM((chunks, 2, PAIR, 2, 2, quarter), f32),
            pltpu.VMEM((chunks, PAIR, 2, HD, quarter), bf),
            pltpu.VMEM((chunks, PAIR, 2, 2, quarter), f32),
            pltpu.VMEM((chunks, 2, PAIR, HD, quarter), bf),
            pltpu.VMEM((chunks, 2, PAIR, 2, quarter), f32),
            pltpu.VMEM((chunks, PAIR, HD, quarter), bf),
            pltpu.VMEM((chunks, PAIR, 2, quarter), f32),
            pltpu.VMEM((chunks, depth, HD, lanes), bf),
            pltpu.VMEM((chunks, depth, 2, lanes), f32),
            pltpu.VMEM((chunks, depth, HD, lanes), bf),
            pltpu.VMEM((chunks, depth, 2, lanes), f32),
            pltpu.VMEM((chunks, HD, lanes), f32),
            pltpu.VMEM((chunks, 2, lanes), f32),
            dma((3,)),
            dma((chunks, depth)), dma((chunks, depth)),
            dma((chunks,)), dma((chunks,)), dma((chunks,)), dma((chunks,)),
            dma((chunks, 2)), dma((chunks, 2)), dma((chunks, 2)), dma((chunks, 2)),
            dma((chunks, depth, 2)), dma((chunks, depth, 2)),
        ],
        compiler_params=pltpu.CompilerParams(
            collective_id=0, has_side_effects=True, vmem_limit_bytes=56 * 1024 * 1024
        ),
    )(query, limit, tail_limit, fresh, root_kv, branch_kv, tail_kv)
    out = out.reshape(KVH, steps, req_here, group, HD)
    return jnp.transpose(out, (1, 2, 0, 3, 4)).reshape(steps, req_here, QH * HD)


def solution(mesh):
    return jax.shard_map(
        body,
        mesh=mesh,
        in_specs=(
            P(None, ("groups", "kv"), None),
            P(None, None, ("groups", "kv"), None),
            P(("groups", "kv"), None, None, None),
            P(("groups", "kv"), None, None, None),
            P(("groups", "kv"), None, None, None),
            P("groups"),
            P("groups"),
            P("groups"),
            P("groups"),
        ),
        out_specs=P(None, ("groups", "kv"), None),
        check_vma=False,
    )
```

time: 254 us -> 69.8 us (0.27)
  the two profiles are of different devices: /device:TPU:13 before, /device:TPU:0 now
where the time goes in v1:
time: 69.8 us; the launch traced here: 69.5 us
  Pallas kernels  59.8 us (86%)
  local copies, waits for them, and re-layouts  6.49 us (9%)
  other arithmetic  3.25 us (5%)
    pallas_call x1, Pallas kernels, body(): pl.pallas_call(functools.partial(kernel, devices, rows, req_here), out_sh...  59.8 us
    reshape x2, local copies, waits for them, and re-layouts, body(): query = queries.reshape(steps, req_here, KVH, group, HD)  1.68 us

profile of v1, /device:TPU:0, one launch (start us, length us, event | category | flops | bytes accessed | tf_op | source)
XLA Modules:
  0.0 69.5 jit_solution(18074103296521947829)
XLA Ops:
  0.0 0.7 %dynamic_slice.6 = s32[4]{0:T(128)S(1)} dynamic-slice(s32[64]{0:T(128)} %param.17, s32[]{:T(128)S(6)} %select_n.50), dynamic_slice_sizes={4} | dynamic-slice | bytes 36 | tf_op jit(solution)/shard_map/dynamic_slice | solution.py:299
  0.7 0.8 %convert_reduce_fusion = s32[4]{0:T(128)S(1)} fusion(s32[4]{0:T(128)S(1)} %iota_add_fusion, s32[64]{0:T(128)} %param.17, s32[4]{0:T(128)S(1)} %dynamic_slice.6), kind=kLoop, calls=%fused_computation.7 | loop fusion | flops 1276 | bytes 304 | tf_op jit(solution)/shard_map/reduce_sum | solution.py:301
  1.6 0.8 %select_reduce_fusion.2 = s32[4]{0:T(128)S(1)} fusion(s32[49]{0:T(128)} %param.15, s32[4]{0:T(128)S(1)} %dynamic_slice.6), kind=kLoop, calls=%fused_computation.9 | loop fusion | flops 584 | bytes 228 | tf_op jit(solution)/shard_map/reduce_sum | solution.py:302
  2.4 0.9 %select_reduce_fusion = (s32[32]{0:T(128)S(1)}, s32[32]{0:T(128)S(1)}) fusion(s32[49]{0:T(128)} %param.15, s32[32]{0:T(128)} %param.16, s32[49]{0:T(128)} %param.14), kind=kLoop, calls=%fused_computation.2 | loop fusion | flops 7776 | bytes 776 | tf_op jit(solution)/shard_map/reduce_sum | solution.py:306
  3.3 0.1 dynamic_slice.7
  3.4 0.6 compare_select_fusion.3.tl_ref
  4.0 0.1 eq.76
  4.1 0.7 %copy.20 = bf16[2,2,2,1024]{3,2,1,0:T(2,128)(2,1)S(1)} copy(bf16[2,2,2,1024]{3,2,0,1:T(2,128)(2,1)} %bitcast.13) | data formatting | bytes 32768 | tf_op jit(solution)/shard_map/transpose | solution.py:319
  4.8 0.1 compare_select_fusion
  4.9 0.6 pad.4.new_ref
  5.6 0.1 broadcast_bitcast_fusion
  5.7 0.8 %reshape.82.lim_ref = s32[2,2,4,256]{3,2,1,0:T(4,128)} reshape(s32[2,2,4,4,2,2,16]{6,5,4,3,2,1,0:T(2,128)S(1)} %broadcast_bitcast_fusion) | data formatting | bytes 32768 | tf_op jit(solution)/shard_map/reshape | solution.py:310
  6.5 1.0 %reshape.80 = bf16[2,2,8,16,128]{4,3,2,1,0:T(8,128)(2,1)S(1)} reshape(bf16[2,2,16384]{2,1,0:T(2,128)(2,1)} %param.9) | data formatting | bytes 262144 | tf_op jit(solution)/shard_map/reshape | solution.py:317
  7.5 0.7 copy.18
  8.2 59.8 %shard_map.91 = bf16[4,128,128]{2,1,0:T(8,128)(2,1)} custom-call(bf16[4,2,64,128]{3,2,1,0:T(8,128)(2,1)} %bitcast.11, s32[2,2,4,256]{3,2,1,0:T(4,128)} %reshape.82.lim_ref, s32[2,128]{1,0:T(2,128)} %compare_select_fusion.3.tl_ref, bf16[2,16,1024]{2,1,0:T(8,128)(2,1)} %pad.4.new_ref, bf16[4,2,128,1024]{3,2,1,0:T(8,128)(2,1)} %root_hbm.1, ...), custom_call_target="tpu_custom_call" | custom-call | tf_op jit(solution)/shard_map/pallas_call | solution.py:328
  67.9 0.9 %copy.21 = bf16[2,2,8,16,128]{4,3,2,1,0:T(8,128)(2,1)S(1)} copy(bf16[2,2,8,16,128]{4,3,1,0,2:T(8,128)(2,1)} %bitcast.12) | data formatting | bytes 262144 | tf_op jit(solution)/shard_map/transpose | solution.py:364
  68.9 0.7 reshape.85
  (5 shorter events, 0.0 us)

commit v2 on v1

--- a/solution.py
+++ b/solution.py
@@ -39,15 +39,18 @@
 
 def kernel(
     devices, rows, req_here,
-    q_ref, lim_ref, tl_ref, new_ref, root_hbm, branch_hbm, tail_hbm,
+    parent, node_len, leaf_of, branch_slot,
+    q_ref, new_ref, root_hbm, branch_hbm, tail_hbm,
     out_ref,
-    qbuf, root, branch, tail, vt,
+    qbuf, root, branch, tail, vt, lim_ref, tl_ref, fresh,
     o1, s1, r1, t1, o2, s2, r2, t2, o3, s3, r3, t3, tacc, tst,
     hbm_sem, agz_s, agz_r, agy_s, agy_r, agc_s, agc_r,
     c_s, c_r, y_s, y_r, z_s, z_r,
 ):
     depth = devices // 4
-    chunks = KVH // PAIR
+    chunks = KVH
+    half_dim = HD // 2
+    group = QH // KVH
     me = lax.axis_index("kv")
     core = lax.rem(me, 2)
     yy = lax.rem(me // 2, 2)
@@ -125,16 +128,62 @@
             gather_z(c, o).start()
         qbuf[c, core, yy, zz] = q_ref[c]
 
+    block_len = root.shape[2]
+    first_slot = me * n_branch
+    slot_nodes = [branch_slot[first_slot + j] for j in range(n_branch)]
+
+    def count_rank(i, ranks):
+        node = branch_slot[i]
+        return tuple(
+            rank + jnp.where((node == slot_nodes[j]) & (i < first_slot + j), 1, 0)
+            for j, rank in enumerate(ranks)
+        )
+
+    ranks = lax.fori_loop(
+        0, branch_slot.shape[0], count_rank, (jnp.int32(0),) * n_branch
+    )
+    fills = []
+    for j in range(n_branch):
+        owned = node_len[jnp.minimum(slot_nodes[j], node_len.shape[0] - 1)]
+        fill = jnp.clip(owned - ranks[j] * block_len, 0, block_len)
+        fills.append(jnp.where(slot_nodes[j] < node_len.shape[0], fill, 0))
+    lane = lax.broadcasted_iota(jnp.int32, (1, quarter), 1)
+    lane_owner = (lane // rows) * req_here + (lane // group) % req_here
+    for half in range(2):
+        for y in range(2):
+            lane_branch = jnp.zeros((1, quarter), jnp.int32)
+            for z in range(depth):
+                for r in range(req_here):
+                    request = ((z * 2 + y) * 2 + half) * req_here + r
+                    lane_branch = jnp.where(
+                        lane_owner == z * req_here + r, parent[leaf_of[request]], lane_branch
+                    )
+            for j in range(n_branch):
+                lim_ref[half, y, j : j + 1, :] = jnp.where(
+                    lane_branch == slot_nodes[j], fills[j], 0
+                )
+    lane = lax.broadcasted_iota(jnp.int32, (1, PAIR * rows), 1)
+    for r in range(req_here):
+        tl_ref[r : r + 1, :] = jnp.where(
+            (lane // group) % req_here == r, node_len[leaf_of[me * req_here + r]], 0
+        )
+    steps = new_ref.shape[0]
+    fresh[...] = jnp.zeros_like(fresh)
+    for s in range(steps):
+        for kv in range(2):
+            fresh[kv, s * req_here : (s + 1) * req_here, :] = new_ref[s, kv]
+
     for load in loads:
         load.wait()
 
     def head_cols(k):
         return pl.ds(pl.multiple_of(k * HD, HD), HD)
 
+    def fold(x, part):
+        return jnp.concatenate([x[:half_dim, part], x[half_dim:, part]], axis=1)
+
     def tail_part(c):
-        lanes = PAIR * rows
-        left = lax.broadcasted_iota(jnp.int32, (1, lanes), 1) < rows
-        query = [q_ref[c, h] for h in range(PAIR)]
+        query = [q_ref[c * PAIR + h] for h in range(PAIR)]
         cols = [head_cols(c * PAIR + h) for h in range(PAIR)]
         scores = []
         for r in range(req_here):
@@ -144,43 +193,44 @@
             token = lax.broadcasted_iota(jnp.int32, s.shape, 0)
             scores.append(jnp.where(token < tl_ref[r : r + 1, :], s, MASKED))
         s = jnp.concatenate(
-            [matmul(new_ref[0, :, cols[h]], query[h], ((1,), (1,))) for h in range(PAIR)], axis=1
+            [matmul(fresh[0, :, cols[h]], query[h], ((1,), (1,))) for h in range(PAIR)], axis=1
         )
         token = lax.broadcasted_iota(jnp.int32, s.shape, 0)
         lane = lax.broadcasted_iota(jnp.int32, s.shape, 1)
-        lane_req = (lane // 16) % req_here
-        lane_step = (lane // (16 * req_here)) % 2
-        live = (token < 2 * req_here) & (token % req_here == lane_req)
+        lane_req = (lane // group) % req_here
+        lane_step = (lane // (group * req_here)) % steps
+        live = (token < steps * req_here) & (token % req_here == lane_req)
         live = live & (token // req_here <= lane_step)
         scores.append(jnp.where(live, s, MASKED))
         top, total, weights = attend(scores)
         outs = []
         for h in range(PAIR):
-            values = [tail[r, 1, :, cols[h]] for r in range(req_here)] + [new_ref[1, :, cols[h]]]
+            values = [tail[r, 1, :, cols[h]] for r in range(req_here)] + [fresh[1, :, cols[h]]]
             outs.append(
                 functools.reduce(
                     jnp.add, [matmul(v, w, ((0,), (0,))) for v, w in zip(values, weights)]
                 )
             )
-        tacc[c] = jnp.where(left, outs[0], outs[1])
-        tst[c] = jnp.concatenate([top, total], axis=0)
+        stat = jnp.concatenate([top, total], axis=0)
+        for h in range(PAIR):
+            part = slice(h * rows, (h + 1) * rows)
+            tacc[c * PAIR + h] = fold(outs[h], part)
+            tst[c * PAIR + h] = jnp.concatenate([stat[:, part]] * 2, axis=1)
 
     def cache_part(c, half):
-        @pl.loop(0, PAIR * 2)
-        def _(i):
-            h, y = i // 2, lax.rem(i, 2)
-            k = c * PAIR + h
-            cols = head_cols(k)
-            query = qbuf[c, half, y, :, h].reshape(quarter, HD)
+        @pl.loop(0, 2)
+        def _(y):
+            cols = head_cols(c)
+            query = qbuf[c, half, y].reshape(quarter, HD)
             scores = [matmul(root[b, 0, :, cols], query, ((1,), (1,))) for b in range(n_root)]
             for b in range(n_branch):
                 s = matmul(branch[b, 0, :, cols], query, ((1,), (1,)))
                 token = lax.broadcasted_iota(jnp.int32, s.shape, 0)
                 scores.append(jnp.where(token < lim_ref[half, y, b : b + 1, :], s, MASKED))
             top, total, weights = attend(scores)
-            out = matmul(vt[k], jnp.concatenate(weights, axis=0), ((1,), (0,)))
-            o1[c, half, h, y] = (out * (1.0 / total)).astype(jnp.bfloat16)
-            s1[c, half, h, y] = jnp.concatenate([top, total], axis=0)
+            out = matmul(vt[c], jnp.concatenate(weights, axis=0), ((1,), (0,)))
+            o1[c, half, y] = (out * (1.0 / total)).astype(jnp.bfloat16)
+            s1[c, half, y] = jnp.concatenate([top, total], axis=0)
 
     @pl.loop(0, KVH)
     def _(k):
@@ -204,10 +254,9 @@
             gather_y(c, 1 - yy).wait_recv()
             gather_c(c, core).start()
 
-        @pl.when(t < chunks // 2)
-        def _():
-            tail_part(2 * t)
-            tail_part(2 * t + 1)
+        @pl.when(t < chunks // PAIR)
+        def _():
+            tail_part(t)
 
         @pl.when((t >= 2) & (t < chunks + 2))
         def _():
@@ -224,10 +273,9 @@
             for copy in send_c(c):
                 copy.wait_recv()
             for y in range(2):
-                for h in range(PAIR):
-                    stat, out = merge(s1[c, core, h, y], o1[c, core, h, y], t1[c, h, y], r1[c, h, y])
-                    o2[c, y, h] = out.astype(jnp.bfloat16)
-                    s2[c, y, h] = stat
+                stat, out = merge(s1[c, core, y], o1[c, core, y], t1[c, y], r1[c, y])
+                o2[c, y] = out.astype(jnp.bfloat16)
+                s2[c, y] = stat
             for copy in send_y(c):
                 copy.start()
 
@@ -236,13 +284,11 @@
             c = t - 4
             for copy in send_y(c):
                 copy.wait_recv()
-            joined = [merge(s2[c, yy, h], o2[c, yy, h], t2[c, h], r2[c, h]) for h in range(PAIR)]
+            stat, out = merge(s2[c, yy], o2[c, yy], t2[c], r2[c])
             for z in range(depth):
                 part = slice(z * rows, (z + 1) * rows)
-                o3[c, z] = jnp.concatenate([j[1][:, part] for j in joined], axis=1).astype(
-                    jnp.bfloat16
-                )
-                s3[c, z] = jnp.concatenate([j[0][:, part] for j in joined], axis=1)
+                o3[c, z] = fold(out, part).astype(jnp.bfloat16)
+                s3[c, z] = jnp.concatenate([stat[:, part]] * 2, axis=1)
             for o in range(1, depth):
                 for copy in send_z(c, o):
                     copy.start()
@@ -264,7 +310,9 @@
                 factor = s[1:2] * jnp.exp2(s[0:1] - top)
                 number = number + o.astype(jnp.float32) * factor
                 total = total + factor
-            out_ref[c] = (number / total).T.astype(jnp.bfloat16)
+            out = number / total
+            out = jnp.concatenate([out[:, :rows], out[:, rows:]], axis=0)
+            out_ref[c] = out.T.astype(jnp.bfloat16)
 
     @pl.loop(0, chunks)
     def _(c):
@@ -280,76 +328,52 @@
 
 def body(queries, new_kv, root_kv, branch_kv, tail_kv, parent, node_len, leaf_of, branch_slot):
     devices = lax.axis_size("kv")
-    device_index = lax.axis_index("kv")
     steps, req_here, _ = queries.shape
-    requests = req_here * devices
     group = QH // KVH
     rows = steps * req_here * group
     depth = devices // 4
     quarter = depth * rows
-    chunks = KVH // PAIR
-    node_count = node_len.shape[0]
-    slot_count = branch_slot.shape[0]
+    chunks = KVH
     slots_here = branch_kv.shape[0]
     block_len = branch_kv.shape[2]
 
-    nodes = jnp.arange(node_count, dtype=jnp.int32)
-    slot_ids = jnp.arange(slot_count, dtype=jnp.int32)
-    local_slots = device_index * slots_here + jnp.arange(slots_here, dtype=jnp.int32)
-    local_node = lax.dynamic_slice(branch_slot, (device_index * slots_here,), (slots_here,))
-    before = slot_ids[None, :] < local_slots[:, None]
-    ranks = jnp.sum(((branch_slot[None, :] == local_node[:, None]) & before).astype(jnp.int32), axis=1)
-    owner_len = jnp.sum(jnp.where(nodes[None, :] == local_node[:, None], node_len[None, :], 0), axis=1)
-    fill = jnp.clip(owner_len - ranks * block_len, 0, block_len)
-    leaf_hot = leaf_of[:, None] == nodes[None, :]
-    request_branch = jnp.sum(jnp.where(leaf_hot, parent[None, :], 0), axis=1)
-    request_tail = jnp.sum(jnp.where(leaf_hot, node_len[None, :], 0), axis=1)
-    limit = jnp.where(request_branch[None, :] == local_node[:, None], fill[:, None], 0)
-    limit = limit.reshape(slots_here, depth, 2, 2, 1, req_here, 1)
-    limit = jnp.broadcast_to(limit, (slots_here, depth, 2, 2, steps, req_here, group))
-    limit = jnp.transpose(limit, (3, 2, 0, 1, 4, 5, 6)).reshape(2, 2, slots_here, quarter)
-    own_tail = lax.dynamic_slice(request_tail, (device_index * req_here,), (req_here,))
-    lane_req = (jnp.arange(PAIR * rows, dtype=jnp.int32) // group) % req_here
-    tail_limit = jnp.where(
-        lane_req[None, :] == jnp.arange(req_here, dtype=jnp.int32)[:, None], own_tail[:, None], 0
-    )
-
     query = queries.reshape(steps, req_here, KVH, group, HD)
-    query = jnp.transpose(query, (2, 0, 1, 3, 4)).reshape(chunks, PAIR, rows, HD)
-    fresh = jnp.swapaxes(new_kv, 0, 1).reshape(2, steps * req_here, KVH * HD)
-    fresh = jnp.pad(fresh, ((0, 0), (0, 16 - steps * req_here), (0, 0)))
-
+    query = jnp.transpose(query, (2, 0, 1, 3, 4)).reshape(KVH, rows, HD)
     bf, f32 = jnp.bfloat16, jnp.float32
     vmem = pl.BlockSpec(memory_space=pltpu.VMEM)
+    smem = pl.BlockSpec(memory_space=pltpu.SMEM)
     hbm = pl.BlockSpec(memory_space=pl.ANY)
     lanes = PAIR * rows
     tokens = (root_kv.shape[0] + slots_here) * block_len
     dma = pltpu.SemaphoreType.DMA
     out = pl.pallas_call(
         functools.partial(kernel, devices, rows, req_here),
-        out_shape=jax.ShapeDtypeStruct((chunks, lanes, HD), bf),
-        in_specs=[vmem] * 4 + [hbm] * 3,
+        out_shape=jax.ShapeDtypeStruct((chunks, rows, HD), bf),
+        in_specs=[smem] * 4 + [vmem] * 2 + [hbm] * 3,
         out_specs=vmem,
         scratch_shapes=[
-            pltpu.VMEM((chunks, 2, 2, depth, PAIR, rows, HD), bf),
+            pltpu.VMEM((chunks, 2, 2, depth, rows, HD), bf),
             pltpu.VMEM(root_kv.shape, bf),
             pltpu.VMEM(branch_kv.shape, bf),
             pltpu.VMEM(tail_kv.shape, bf),
             pltpu.VMEM((KVH, HD, tokens), bf),
-            pltpu.VMEM((chunks, 2, PAIR, 2, HD, quarter), bf),
-            pltpu.VMEM((chunks, 2, PAIR, 2, 2, quarter), f32),
-            pltpu.VMEM((chunks, PAIR, 2, HD, quarter), bf),
-            pltpu.VMEM((chunks, PAIR, 2, 2, quarter), f32),
-            pltpu.VMEM((chunks, 2, PAIR, HD, quarter), bf),
-            pltpu.VMEM((chunks, 2, PAIR, 2, quarter), f32),
-            pltpu.VMEM((chunks, PAIR, HD, quarter), bf),
-            pltpu.VMEM((chunks, PAIR, 2, quarter), f32),
-            pltpu.VMEM((chunks, depth, HD, lanes), bf),
-            pltpu.VMEM((chunks, depth, 2, lanes), f32),
-            pltpu.VMEM((chunks, depth, HD, lanes), bf),
-            pltpu.VMEM((chunks, depth, 2, lanes), f32),
-            pltpu.VMEM((chunks, HD, lanes), f32),
-            pltpu.VMEM((chunks, 2, lanes), f32),
+            pltpu.VMEM((2, 2, slots_here, quarter), jnp.int32),
+            pltpu.VMEM((req_here, lanes), jnp.int32),
+            pltpu.VMEM((2, 16, KVH * HD), bf),
+            pltpu.VMEM((chunks, 2, 2, HD, quarter), bf),
+            pltpu.VMEM((chunks, 2, 2, 2, quarter), f32),
+            pltpu.VMEM((chunks, 2, HD, quarter), bf),
+            pltpu.VMEM((chunks, 2, 2, quarter), f32),
+            pltpu.VMEM((chunks, 2, HD, quarter), bf),
+            pltpu.VMEM((chunks, 2, 2, quarter), f32),
+            pltpu.VMEM((chunks, HD, quarter), bf),
+            pltpu.VMEM((chunks, 2, quarter), f32),
+            pltpu.VMEM((chunks, depth, HD // 2, 2 * rows), bf),
+            pltpu.VMEM((chunks, depth, 2, 2 * rows), f32),
+            pltpu.VMEM((chunks, depth, HD // 2, 2 * rows), bf),
+            pltpu.VMEM((chunks, depth, 2, 2 * rows), f32),
+            pltpu.VMEM((chunks, HD // 2, 2 * rows), f32),
+            pltpu.VMEM((chunks, 2, 2 * rows), f32),
             dma((3,)),
             dma((chunks, depth)), dma((chunks, depth)),
             dma((chunks,)), dma((chunks,)), dma((chunks,)), dma((chunks,)),
@@ -359,7 +383,7 @@
         compiler_params=pltpu.CompilerParams(
             collective_id=0, has_side_effects=True, vmem_limit_bytes=56 * 1024 * 1024
         ),
-    )(query, limit, tail_limit, fresh, root_kv, branch_kv, tail_kv)
+    )(parent, node_len, leaf_of, branch_slot, query, new_kv, root_kv, branch_kv, tail_kv)
     out = out.reshape(KVH, steps, req_here, group, HD)
     return jnp.transpose(out, (1, 2, 0, 3, 4)).reshape(steps, req_here, QH * HD)
 

time: 69.8 us -> 62.1 us (0.89)
  other arithmetic: 3.25 us -> 0 us
  local copies, waits for them, and re-layouts: 6.49 us -> 3.28 us
  Pallas kernels: 59.8 us -> 58.6 us
    reduce_sum x3 -> x0, other arithmetic: 2.54 us -> none  [the longest x1 0.87 us: body(): request_tail = jnp.sum(jnp.where(leaf_hot, node_len[None, :], 0), axis=1)]
    pallas_call x1, Pallas kernels: 59.8 us -> 58.6 us  [body(): pl.pallas_call(functools.partial(kernel, devices, rows, req_here), out_sh...]
    transpose x2 -> x0, local copies, waits for them, and re-layouts: 0.86 us -> none  [the longest x1 0.73 us: body(): fresh = jnp.swapaxes(new_kv, 0, 1).reshape(2, steps * req_here, KVH * HD)]
    reshape x2 -> x0, local copies, waits for them, and re-layouts: 0.82 us -> none  [the longest x1 0.8 us: body(): jnp.transpose(limit, (3, 2, 0, 1, 4, 5, 6))]
    dynamic_slice x2 -> x0, local copies, waits for them, and re-layouts: 0.8 us -> none  [the longest x1 0.73 us: body(): lax.dynamic_slice(branch_slot, (device_index * slots_here,), (slots_here,))]
where the time goes in v2:
time: 62.1 us; the launch traced here: 61.9 us
  Pallas kernels  58.6 us (94%)
  local copies, waits for them, and re-layouts  3.28 us (5%)
    pallas_call x1, Pallas kernels, body(): pl.pallas_call(functools.partial(kernel, devices, rows, req_here), out_sh...  58.6 us
    reshape x2, local copies, waits for them, and re-layouts, body(): query = queries.reshape(steps, req_here, KVH, group, HD)  1.68 us

profile of v2, /device:TPU:0, one launch (start us, length us, event | category | flops | bytes accessed | tf_op | source)
XLA Modules:
  0.0 61.9 jit_solution(15644993110547425256)
XLA Ops:
  0.0 1.0 %reshape.12 = bf16[2,2,8,16,128]{4,3,2,1,0:T(8,128)(2,1)S(1)} reshape(bf16[2,2,16384]{2,1,0:T(2,128)(2,1)} %param.9) | data formatting | bytes 262144 | tf_op jit(solution)/shard_map/reshape | solution.py:340
  1.0 0.7 %copy.10 = bf16[2,2,8,16,128]{4,3,1,0,2:T(8,128)(2,1)} copy(bf16[2,2,8,16,128]{4,3,2,1,0:T(8,128)(2,1)S(1)} %reshape.12) | data formatting | bytes 262144 | tf_op jit(solution)/shard_map/reshape | solution.py:340
  1.7 58.6 %shard_map.91 = bf16[8,64,128]{2,1,0:T(8,128)(2,1)} custom-call(s32[49]{0:T(128)} %parent.1, s32[49]{0:T(128)} %node_len.1, s32[32]{0:T(128)} %leaf_of.1, s32[64]{0:T(128)} %branch_slot.1, bf16[8,64,128]{2,1,0:T(8,128)(2,1)} %bitcast.8, bf16[2,2,2,1024]{3,2,1,0:T(2,128)(2,1)} %new_ref.1, bf16[4,2,128,1024]{3,2,1,0:T(8,128)(2,1)} %root_hbm.1, ...), custom_call_target="tpu_custom_call" | custom-call | tf_op jit(solution)/shard_map/pallas_call | solution.py:349
  60.3 0.9 %copy.11 = bf16[2,2,8,16,128]{4,3,2,1,0:T(8,128)(2,1)S(1)} copy(bf16[2,2,8,16,128]{4,3,1,0,2:T(8,128)(2,1)} %bitcast.9) | data formatting | bytes 262144 | tf_op jit(solution)/shard_map/transpose | solution.py:388
  61.2 0.7 %reshape.15 = bf16[2,2,16384]{2,1,0:T(2,128)(2,1)} reshape(bf16[2,2,8,16,128]{4,3,2,1,0:T(8,128)(2,1)S(1)} %copy.11) | data formatting | bytes 262144 | tf_op jit(solution)/shard_map/reshape | solution.py:388

commit v3 on v2

--- a/solution.py
+++ b/solution.py
@@ -13,6 +13,11 @@
 PAIR = 2
 MASKED = -1e30
 LOG2E = 1.4426950408889634
+LAG_Y = 2
+LAG_CORE = 3
+LAG_OUT_CORE = 4
+LAG_OUT_Y = 6
+LAG_LAST = 8
 
 
 def attend(scores):
@@ -60,6 +65,7 @@
     n_root = root.shape[0]
     n_branch = branch.shape[0]
     quarter = depth * rows
+    steps = new_ref.shape[0]
 
     def z_peer(offset):
         z = lax.rem(zz + offset, depth)
@@ -128,53 +134,50 @@
             gather_z(c, o).start()
         qbuf[c, core, yy, zz] = q_ref[c]
 
-    block_len = root.shape[2]
-    first_slot = me * n_branch
-    slot_nodes = [branch_slot[first_slot + j] for j in range(n_branch)]
-
-    def count_rank(i, ranks):
-        node = branch_slot[i]
-        return tuple(
-            rank + jnp.where((node == slot_nodes[j]) & (i < first_slot + j), 1, 0)
-            for j, rank in enumerate(ranks)
-        )
-
-    ranks = lax.fori_loop(
-        0, branch_slot.shape[0], count_rank, (jnp.int32(0),) * n_branch
-    )
-    fills = []
-    for j in range(n_branch):
-        owned = node_len[jnp.minimum(slot_nodes[j], node_len.shape[0] - 1)]
-        fill = jnp.clip(owned - ranks[j] * block_len, 0, block_len)
-        fills.append(jnp.where(slot_nodes[j] < node_len.shape[0], fill, 0))
-    lane = lax.broadcasted_iota(jnp.int32, (1, quarter), 1)
-    lane_owner = (lane // rows) * req_here + (lane // group) % req_here
-    for half in range(2):
-        for y in range(2):
-            lane_branch = jnp.zeros((1, quarter), jnp.int32)
-            for z in range(depth):
-                for r in range(req_here):
-                    request = ((z * 2 + y) * 2 + half) * req_here + r
-                    lane_branch = jnp.where(
-                        lane_owner == z * req_here + r, parent[leaf_of[request]], lane_branch
+    def tables():
+        block_len = root.shape[2]
+        first_slot = me * n_branch
+        slot_nodes = [branch_slot[first_slot + j] for j in range(n_branch)]
+
+        def count_rank(i, ranks):
+            node = branch_slot[i]
+            return tuple(
+                rank + jnp.where((node == slot_nodes[j]) & (i < first_slot + j), 1, 0)
+                for j, rank in enumerate(ranks)
+            )
+
+        ranks = lax.fori_loop(
+            0, branch_slot.shape[0], count_rank, (jnp.int32(0),) * n_branch
+        )
+        fills = []
+        for j in range(n_branch):
+            owned = node_len[jnp.minimum(slot_nodes[j], node_len.shape[0] - 1)]
+            fill = jnp.clip(owned - ranks[j] * block_len, 0, block_len)
+            fills.append(jnp.where(slot_nodes[j] < node_len.shape[0], fill, 0))
+        lane = lax.broadcasted_iota(jnp.int32, (1, quarter), 1)
+        lane_owner = (lane // rows) * req_here + (lane // group) % req_here
+        for half in range(2):
+            for y in range(2):
+                lane_branch = jnp.zeros((1, quarter), jnp.int32)
+                for z in range(depth):
+                    for r in range(req_here):
+                        request = ((z * 2 + y) * 2 + half) * req_here + r
+                        lane_branch = jnp.where(
+                            lane_owner == z * req_here + r, parent[leaf_of[request]], lane_branch
+                        )
+                for j in range(n_branch):
+                    lim_ref[half, y, j : j + 1, :] = jnp.where(
+                        lane_branch == slot_nodes[j], fills[j], 0
                     )
-            for j in range(n_branch):
-                lim_ref[half, y, j : j + 1, :] = jnp.where(
-                    lane_branch == slot_nodes[j], fills[j], 0
-                )
-    lane = lax.broadcasted_iota(jnp.int32, (1, PAIR * rows), 1)
-    for r in range(req_here):
-        tl_ref[r : r + 1, :] = jnp.where(
-            (lane // group) % req_here == r, node_len[leaf_of[me * req_here + r]], 0
-        )
-    steps = new_ref.shape[0]
-    fresh[...] = jnp.zeros_like(fresh)
-    for s in range(steps):
-        for kv in range(2):
-            fresh[kv, s * req_here : (s + 1) * req_here, :] = new_ref[s, kv]
-
-    for load in loads:
-        load.wait()
+        lane = lax.broadcasted_iota(jnp.int32, (1, PAIR * rows), 1)
+        for r in range(req_here):
+            tl_ref[r : r + 1, :] = jnp.where(
+                (lane // group) % req_here == r, node_len[leaf_of[me * req_here + r]], 0
+            )
+        fresh[...] = jnp.zeros_like(fresh)
+        for s in range(steps):
+            for kv in range(2):
+                fresh[kv, s * req_here : (s + 1) * req_here, :] = new_ref[s, kv]
 
     def head_cols(k):
         return pl.ds(pl.multiple_of(k * HD, HD), HD)
@@ -232,15 +235,14 @@
             o1[c, half, y] = (out * (1.0 / total)).astype(jnp.bfloat16)
             s1[c, half, y] = jnp.concatenate([top, total], axis=0)
 
-    @pl.loop(0, KVH)
-    def _(k):
+    def turn_values(k):
         cols = head_cols(k)
         for b in range(n_root):
             vt[k, :, b * HD : (b + 1) * HD] = root[b, 1, :, cols].T
         for b in range(n_branch):
             vt[k, :, (n_root + b) * HD : (n_root + b + 1) * HD] = branch[b, 1, :, cols].T
 
-    @pl.loop(0, chunks + 5)
+    @pl.loop(0, chunks + LAG_LAST)
     def _(t):
         @pl.when(t < chunks)
         def _():
@@ -248,28 +250,36 @@
                 gather_z_in(t, o).wait_recv()
             gather_y(t, yy).start()
 
-        @pl.when((t >= 1) & (t < chunks + 1))
-        def _():
-            c = t - 1
+        @pl.when((t >= LAG_Y) & (t < chunks + LAG_Y))
+        def _():
+            c = t - LAG_Y
             gather_y(c, 1 - yy).wait_recv()
             gather_c(c, core).start()
 
+        @pl.when(t == 0)
+        def _():
+            tables()
+            for load in loads:
+                load.wait()
+
         @pl.when(t < chunks // PAIR)
         def _():
+            turn_values(PAIR * t)
+            turn_values(PAIR * t + 1)
             tail_part(t)
 
-        @pl.when((t >= 2) & (t < chunks + 2))
-        def _():
-            c = t - 2
+        @pl.when((t >= LAG_CORE) & (t < chunks + LAG_CORE))
+        def _():
+            c = t - LAG_CORE
             gather_c(c, 1 - core).wait_recv()
             cache_part(c, 1 - core)
             for copy in send_c(c):
                 copy.start()
             cache_part(c, core)
 
-        @pl.when((t >= 3) & (t < chunks + 3))
-        def _():
-            c = t - 3
+        @pl.when((t >= LAG_OUT_CORE) & (t < chunks + LAG_OUT_CORE))
+        def _():
+            c = t - LAG_OUT_CORE
             for copy in send_c(c):
                 copy.wait_recv()
             for y in range(2):
@@ -279,9 +289,9 @@
             for copy in send_y(c):
                 copy.start()
 
-        @pl.when((t >= 4) & (t < chunks + 4))
-        def _():
-            c = t - 4
+        @pl.when((t >= LAG_OUT_Y) & (t < chunks + LAG_OUT_Y))
+        def _():
+            c = t - LAG_OUT_Y
             for copy in send_y(c):
                 copy.wait_recv()
             stat, out = merge(s2[c, yy], o2[c, yy], t2[c], r2[c])
@@ -293,9 +303,9 @@
                 for copy in send_z(c, o):
                     copy.start()
 
-        @pl.when(t >= 5)
-        def _():
-            c = t - 5
+        @pl.when(t >= LAG_LAST)
+        def _():
+            c = t - LAG_LAST
             for o in range(1, depth):
                 for copy in send_z(c, o):
                     copy.wait_recv()

time: 62.1 us -> 59.8 us (0.963)
  Pallas kernels: 58.6 us -> 56.3 us
    pallas_call x1, Pallas kernels: 58.6 us -> 56.3 us  [body(): pl.pallas_call(functools.partial(kernel, devices, rows, req_here), out_sh...]
where the time goes in v3:
time: 59.8 us; the launch traced here: 59.6 us
  Pallas kernels  56.3 us (94%)
  local copies, waits for them, and re-layouts  3.28 us (5%)
    pallas_call x1, Pallas kernels, body(): pl.pallas_call(functools.partial(kernel, devices, rows, req_here), out_sh...  56.3 us
    reshape x2, local copies, waits for them, and re-layouts, body(): query = queries.reshape(steps, req_here, KVH, group, HD)  1.68 us

profile of v3, /device:TPU:0, one launch (start us, length us, event | category | flops | bytes accessed | tf_op | source)
XLA Modules:
  0.0 59.6 jit_solution(17941236276636881545)
XLA Ops:
  0.0 1.0 %reshape.12 = bf16[2,2,8,16,128]{4,3,2,1,0:T(8,128)(2,1)S(1)} reshape(bf16[2,2,16384]{2,1,0:T(2,128)(2,1)} %param.9) | data formatting | bytes 262144 | tf_op jit(solution)/shard_map/reshape | solution.py:350
  1.0 0.7 %copy.10 = bf16[2,2,8,16,128]{4,3,1,0,2:T(8,128)(2,1)} copy(bf16[2,2,8,16,128]{4,3,2,1,0:T(8,128)(2,1)S(1)} %reshape.12) | data formatting | bytes 262144 | tf_op jit(solution)/shard_map/reshape | solution.py:350
  1.7 56.3 %shard_map.91 = bf16[8,64,128]{2,1,0:T(8,128)(2,1)} custom-call(s32[49]{0:T(128)} %parent.1, s32[49]{0:T(128)} %node_len.1, s32[32]{0:T(128)} %leaf_of.1, s32[64]{0:T(128)} %branch_slot.1, bf16[8,64,128]{2,1,0:T(8,128)(2,1)} %bitcast.8, bf16[2,2,2,1024]{3,2,1,0:T(2,128)(2,1)} %new_ref.1, bf16[4,2,128,1024]{3,2,1,0:T(8,128)(2,1)} %root_hbm.1, ...), custom_call_target="tpu_custom_call" | custom-call | tf_op jit(solution)/shard_map/pallas_call | solution.py:359
  58.0 0.9 %copy.11 = bf16[2,2,8,16,128]{4,3,2,1,0:T(8,128)(2,1)S(1)} copy(bf16[2,2,8,16,128]{4,3,1,0,2:T(8,128)(2,1)} %bitcast.9) | data formatting | bytes 262144 | tf_op jit(solution)/shard_map/transpose | solution.py:398
  58.9 0.7 %reshape.15 = bf16[2,2,16384]{2,1,0:T(2,128)(2,1)} reshape(bf16[2,2,8,16,128]{4,3,2,1,0:T(8,128)(2,1)S(1)} %copy.11) | data formatting | bytes 262144 | tf_op jit(solution)/shard_map/reshape | solution.py:398

commit v4 on v3

--- a/solution.py
+++ b/solution.py
@@ -221,7 +221,7 @@
             tst[c * PAIR + h] = jnp.concatenate([stat[:, part]] * 2, axis=1)
 
     def cache_part(c, half):
-        @pl.loop(0, 2)
+        @pl.loop(0, 2, unroll=True)
         def _(y):
             cols = head_cols(c)
             query = qbuf[c, half, y].reshape(quarter, HD)

time: 59.8 us -> 55.7 us (0.931)
  Pallas kernels: 56.3 us -> 52.2 us
    pallas_call x1, Pallas kernels: 56.3 us -> 52.2 us  [body(): pl.pallas_call(functools.partial(kernel, devices, rows, req_here), out_sh...]
where the time goes in v4:
time: 55.7 us; the launch traced here: 55.5 us
  Pallas kernels  52.2 us (94%)
  local copies, waits for them, and re-layouts  3.28 us (6%)
    pallas_call x1, Pallas kernels, body(): pl.pallas_call(functools.partial(kernel, devices, rows, req_here), out_sh...  52.2 us
    reshape x2, local copies, waits for them, and re-layouts, body(): query = queries.reshape(steps, req_here, KVH, group, HD)  1.68 us

profile of v4, /device:TPU:0, one launch (start us, length us, event | category | flops | bytes accessed | tf_op | source)
XLA Modules:
  0.0 55.5 jit_solution(14740841757666146273)
XLA Ops:
  0.0 1.0 %reshape.12 = bf16[2,2,8,16,128]{4,3,2,1,0:T(8,128)(2,1)S(1)} reshape(bf16[2,2,16384]{2,1,0:T(2,128)(2,1)} %param.9) | data formatting | bytes 262144 | tf_op jit(solution)/shard_map/reshape | solution.py:350
  1.0 0.7 %copy.10 = bf16[2,2,8,16,128]{4,3,1,0,2:T(8,128)(2,1)} copy(bf16[2,2,8,16,128]{4,3,2,1,0:T(8,128)(2,1)S(1)} %reshape.12) | data formatting | bytes 262144 | tf_op jit(solution)/shard_map/reshape | solution.py:350
  1.7 52.2 %shard_map.91 = bf16[8,64,128]{2,1,0:T(8,128)(2,1)} custom-call(s32[49]{0:T(128)} %parent.1, s32[49]{0:T(128)} %node_len.1, s32[32]{0:T(128)} %leaf_of.1, s32[64]{0:T(128)} %branch_slot.1, bf16[8,64,128]{2,1,0:T(8,128)(2,1)} %bitcast.8, bf16[2,2,2,1024]{3,2,1,0:T(2,128)(2,1)} %new_ref.1, bf16[4,2,128,1024]{3,2,1,0:T(8,128)(2,1)} %root_hbm.1, ...), custom_call_target="tpu_custom_call" | custom-call | tf_op jit(solution)/shard_map/pallas_call | solution.py:359
  53.9 0.9 %copy.11 = bf16[2,2,8,16,128]{4,3,2,1,0:T(8,128)(2,1)S(1)} copy(bf16[2,2,8,16,128]{4,3,1,0,2:T(8,128)(2,1)} %bitcast.9) | data formatting | bytes 262144 | tf_op jit(solution)/shard_map/transpose | solution.py:398
  54.8 0.7 %reshape.15 = bf16[2,2,16384]{2,1,0:T(2,128)(2,1)} reshape(bf16[2,2,8,16,128]{4,3,2,1,0:T(8,128)(2,1)S(1)} %copy.11) | data formatting | bytes 262144 | tf_op jit(solution)/shard_map/reshape | solution.py:398
